TPU v7x, 256 devices: a whole 4x4x8 slice. The times are simulated.
256 devices in a mesh: ctx: 8 (over z), exp: 32 (over y, x, core).
Axes of the slice: x: 4, y: 4, z: 8, core: 2. Of those that a mesh axis runs over, the one named last changes fastest.
Arguments:
- query_rows: bfloat16 [6144, 4096], P('ctx', 'exp'), may hold values from -6 to 6
- key_rows: bfloat16 [6144, 4096], P('ctx', 'exp'), may hold values from -6 to 6
- value_rows: bfloat16 [6144, 4096], P('ctx', 'exp'), may hold values from -6 to 6
- log_decay: float32 [32, 6144], P('exp', 'ctx'), may hold values from -1 to 0
- residual: bfloat16 [6144, 3072], P(('ctx', 'exp')), may hold values from -20 to 20
- norm_gain: float32 [3072], replicated, may hold values from 0.1 to 1.9
- out_grad: bfloat16 [6144, 3072], P(('ctx', 'exp')), may hold values from -6 to 6
- experts_of: int32 [6144, 2], P(('ctx', 'exp')), may hold values from 0 to 31, all different within a row; in each aligned block of 24 rows (0 to 23, 24 to 47, ...) at most 2 rows name the same one
- route_weight: float32 [6144, 2], P(('ctx', 'exp')), may hold values from 0.1 to 0.9
- output_weight: bfloat16 [4096, 3072], P('exp'), may hold values from -0.09375 to 0.09375
- expert_gate: bfloat16 [32, 3072, 4608], P('exp', None, 'ctx'), may hold values from -0.109375 to 0.109375
- expert_up: bfloat16 [32, 3072, 4608], P('exp', None, 'ctx'), may hold values from -0.109375 to 0.109375
- expert_down: bfloat16 [32, 4608, 3072], P('exp', 'ctx'), may hold values from -0.09375 to 0.09375
Outputs:
- query_grad: bfloat16 [6144, 4096], P('ctx', 'exp')
- key_grad: bfloat16 [6144, 4096], P('ctx', 'exp')
- value_grad: bfloat16 [6144, 4096], P('ctx', 'exp')
Inputs may be any that keep to these rules, and one draw needn't show every extreme that they name: `experts_of`: in each aligned block of 24 tokens (the tokens of one device) no expert is named by more than 2 tokens, a bound that some block reaches; a token's two experts differ.
All inputs are finite; a program needn't handle non-finite values.
Results may differ from a plain program's by a relative error of at most 0.017.
Values may be sent and summed in bfloat16 or wider, within the bound.
No kernel may reach another device: no remote copies, remote signals or barrier semaphores. Data moves between devices by JAX's collectives and lax.ppermute only.
A program may use at most 128 MiB of HBM per device.

v0:
```python
import math
import jax
import jax.numpy as jnp
from jax import lax
from jax.sharding import PartitionSpec as P


def prefix(part, axis, combine, identity, reverse):
    count = lax.axis_size(axis)
    place = lax.axis_index(axis)
    ahead = count - 1 - place if reverse else place
    gathered = jax.tree.map(lambda a: lax.all_gather(a, axis), part)
    state = jax.tree.map(lambda a, e: jnp.zeros_like(a) + jnp.asarray(e, a.dtype), part, identity)

    def one(turn, state):
        source = count - 1 - turn if reverse else turn
        return combine(
            state, jax.tree.map(lambda a: lax.dynamic_index_in_dim(a, source, 0, False), gathered)
        )

    return lax.fori_loop(0, ahead, one, state)


def normalize(residual, norm_gain):
    residual_f = residual.astype(jnp.float32)
    factor = lax.rsqrt(jnp.mean(residual_f * residual_f, axis=-1, keepdims=True) + 1e-05)
    return (residual_f, factor, (residual_f * factor * norm_gain).astype(jnp.bfloat16))


def slot_table(experts_of, count, capacity):
    flat_ids = experts_of.reshape(-1)
    matches = (flat_ids[:, None] == jnp.arange(count, dtype=jnp.int32)[None, :]).astype(jnp.int32)
    before = jnp.cumsum(matches, axis=0, dtype=jnp.int32) - matches
    target = flat_ids * capacity + jnp.sum(before * matches, axis=1, dtype=jnp.int32)
    slots = jnp.arange(count * capacity, dtype=jnp.int32)
    return (slots[:, None] == target[None, :]).astype(jnp.bfloat16)


def expert_rows(row_block, gate_mat, up_mat, down_mat):
    features = gate_mat.shape[0]
    row_input = row_block[:, :features]
    row_grad = row_block[:, features:]
    gate_pre = jnp.dot(row_input, gate_mat, preferred_element_type=jnp.float32)
    up_pre = jnp.dot(row_input, up_mat, preferred_element_type=jnp.float32)
    hidden_grad = lax.dot_general(
        row_grad, down_mat, (((1,), (1,)), ((), ())), preferred_element_type=jnp.float32
    )
    gate_sig = jax.nn.sigmoid(gate_pre)
    gate_grad = (hidden_grad * up_pre * gate_sig * (1.0 + gate_pre * (1.0 - gate_sig))).astype(
        jnp.bfloat16
    )
    up_grad = (hidden_grad * gate_pre * gate_sig).astype(jnp.bfloat16)
    first = lax.dot_general(
        gate_grad, gate_mat, (((1,), (1,)), ((), ())), preferred_element_type=jnp.float32
    )
    second = lax.dot_general(
        up_grad, up_mat, (((1,), (1,)), ((), ())), preferred_element_type=jnp.float32
    )
    return first + second


def block_terms(query_part, key_part, value_part, grad_part, log_steps, score_scale):
    levels = jnp.cumsum(log_steps)
    block_total = levels[-1]
    from_start = jnp.exp(levels)
    to_end = jnp.exp(block_total - levels)
    key_state = lax.dot_general(
        key_part.astype(jnp.float32) * to_end[:, None],
        value_part.astype(jnp.float32),
        (((0,), (0,)), ((), ())),
        precision=lax.Precision.HIGHEST,
    )
    adjoint = score_scale * lax.dot_general(
        query_part.astype(jnp.float32) * from_start[:, None],
        grad_part.astype(jnp.float32),
        (((0,), (0,)), ((), ())),
        precision=lax.Precision.HIGHEST,
    )
    return (levels, jnp.exp(block_total), key_state, adjoint)


def block_grads(
    query_part, key_part, value_part, grad_part, levels, state_in, adjoint_out, score_scale
):
    block_total = levels[-1]
    from_start = jnp.exp(levels)
    to_end = jnp.exp(block_total - levels)
    token_position = jnp.arange(levels.shape[0], dtype=jnp.int32)
    causal = token_position[:, None] >= token_position[None, :]
    fading = jnp.exp(jnp.where(causal, levels[:, None] - levels[None, :], -jnp.inf))
    scores = lax.dot_general(
        query_part, key_part, (((1,), (1,)), ((), ())), preferred_element_type=jnp.float32
    )
    attn_probs = (score_scale * scores * fading).astype(jnp.bfloat16)
    grad_scores = lax.dot_general(
        grad_part, value_part, (((1,), (1,)), ((), ())), preferred_element_type=jnp.float32
    )
    pull_weights = (score_scale * grad_scores * fading).astype(jnp.bfloat16)
    grad_f = grad_part.astype(jnp.float32)
    query_out = jnp.dot(pull_weights, key_part, preferred_element_type=jnp.float32)
    query_out = query_out + score_scale * from_start[:, None] * lax.dot_general(
        grad_f, state_in, (((1,), (1,)), ((), ())), precision=lax.Precision.HIGHEST
    )
    key_out = lax.dot_general(
        pull_weights, query_part, (((0,), (0,)), ((), ())), preferred_element_type=jnp.float32
    )
    key_out = key_out + to_end[:, None] * lax.dot_general(
        value_part.astype(jnp.float32),
        adjoint_out,
        (((1,), (1,)), ((), ())),
        precision=lax.Precision.HIGHEST,
    )
    value_out = lax.dot_general(
        attn_probs, grad_part, (((0,), (0,)), ((), ())), preferred_element_type=jnp.float32
    )
    value_out = value_out + to_end[:, None] * jnp.dot(
        key_part.astype(jnp.float32), adjoint_out, precision=lax.Precision.HIGHEST
    )
    return (
        query_out.astype(jnp.bfloat16),
        key_out.astype(jnp.bfloat16),
        value_out.astype(jnp.bfloat16),
    )


def chain_link(earlier, following):
    return (earlier[0] * following[0], following[0] * earlier[1] + following[1])


def body(
    query_rows,
    key_rows,
    value_rows,
    log_decay,
    residual,
    norm_gain,
    out_grad,
    experts_of,
    route_weight,
    output_weight,
    expert_gate,
    expert_up,
    expert_down,
):
    ctx_count = lax.axis_size("ctx")
    exp_count = lax.axis_size("exp")
    token_count = residual.shape[0]
    features = residual.shape[1]
    capacity = max(2, 3 * token_count // exp_count)
    residual_f, factor, expert_input = normalize(residual, norm_gain)
    slot_onehot = slot_table(experts_of, exp_count, capacity)
    routed = (route_weight[:, :, None] * out_grad.astype(jnp.float32)[:, None, :]).astype(
        jnp.bfloat16
    )
    inputs = jnp.broadcast_to(expert_input[:, None, :], routed.shape)
    packed = jnp.concatenate([inputs, routed], axis=-1).reshape(2 * token_count, 2 * features)
    outgoing = jnp.dot(slot_onehot, packed, preferred_element_type=jnp.float32).astype(jnp.bfloat16)
    outgoing = outgoing.reshape(exp_count, capacity, 2 * features)
    gate_mat = expert_gate[0]
    up_mat = expert_up[0]
    down_mat = expert_down[0]
    arrived = lax.all_to_all(outgoing, "exp", split_axis=0, concat_axis=0, tiled=True).reshape(
        exp_count * capacity, 2 * features
    )
    partials = expert_rows(
        lax.all_gather(arrived, "ctx", axis=0, tiled=True), gate_mat, up_mat, down_mat
    )
    partials = partials.reshape(ctx_count, exp_count, capacity, features)
    summed = lax.psum_scatter(
        partials.astype(jnp.bfloat16), "ctx", scatter_dimension=0, tiled=True
    ).astype(jnp.float32)
    returned = lax.all_to_all(
        summed[0].astype(jnp.bfloat16), "exp", split_axis=0, concat_axis=0, tiled=True
    )
    per_row = lax.dot_general(
        slot_onehot,
        returned.reshape(exp_count * capacity, features),
        (((0,), (0,)), ((), ())),
        preferred_element_type=jnp.float32,
    )
    moe_grad = jnp.sum(per_row.reshape(token_count, 2, features), axis=1)
    scaled = norm_gain * moe_grad
    unit_rows = residual_f * factor
    total_grad = out_grad.astype(jnp.float32) + factor * (
        scaled - unit_rows * jnp.mean(unit_rows * scaled, axis=-1, keepdims=True)
    )
    resid_grad = total_grad.astype(jnp.bfloat16)
    attn_grad = lax.dot_general(
        lax.all_gather(resid_grad, "exp", axis=0, tiled=True),
        output_weight,
        (((1,), (1,)), ((), ())),
        preferred_element_type=jnp.float32,
    ).astype(jnp.bfloat16)
    block_len = query_rows.shape[0]
    head_size = query_rows.shape[1]
    score_scale = 1.0 / math.sqrt(head_size * block_len * ctx_count)
    levels, block_gain, key_state, adjoint = block_terms(
        query_rows, key_rows, value_rows, attn_grad, log_decay[0], score_scale
    )
    zero_state = jnp.zeros((head_size, head_size), jnp.float32)
    identity = (jnp.ones((), jnp.float32), zero_state)
    state_pair = prefix((block_gain, key_state), "ctx", chain_link, identity, False)
    adjoint_pair = prefix((block_gain, adjoint), "ctx", chain_link, identity, True)
    state_in = state_pair[1]
    adjoint_out = adjoint_pair[1]
    return block_grads(
        query_rows, key_rows, value_rows, attn_grad, levels, state_in, adjoint_out, score_scale
    )


def solution(mesh):
    placed = (
        P("ctx", "exp"),
        P("ctx", "exp"),
        P("ctx", "exp"),
        P("exp", "ctx"),
        P(("ctx", "exp"), None),
        P(),
        P(("ctx", "exp"), None),
        P(("ctx", "exp"), None),
        P(("ctx", "exp"), None),
        P("exp", None),
        P("exp", None, "ctx"),
        P("exp", None, "ctx"),
        P("exp", "ctx", None),
    )
    return jax.shard_map(
        body,
        mesh=mesh,
        in_specs=placed,
        out_specs=(P("ctx", "exp"), P("ctx", "exp"), P("ctx", "exp")),
        check_vma=False,
    )
```

profile of v0, /device:TPU:2, one launch (start us, length us, event | category | flops | bytes accessed | tf_op | source)
XLA Modules:
  0.0 386.1 jit_solution(18143667295432726540)
XLA Ops:
  18.4 2.3 mul.203
  23.2 2.2 convolution_convert_fusion
  25.4 2.9 reshape.141
  28.3 20.9 %all_to_all.10 = bf16[32,2,6144]{2,1,0:T(2,128)(2,1)} all-to-all(bf16[32,2,6144]{2,1,0:T(2,128)(2,1)} %reshape.141), channel_id=1, replica_groups=mesh['ctx'=8,'exp'=32] {'exp'}, dimensions={0} | all-to-all | bytes 1572864 | tf_op jit(solution)/shard_map/all_to_all | solution.py:162
  49.2 3.0 reshape.142
  52.4 74.6 %all-gather.5.cloned.1.call-done = bf16[512,6144]{1,0:T(8,128)(2,1)} async-done(((bf16[64,6144]{1,0:T(8,128)(2,1)}), bf16[512,6144]{1,0:T(8,128)(2,1)}) %all-gather.5.cloned.1.call-update) | async-done | bytes 6291472 | tf_op jit(solution)/shard_map/all_gather | solution.py:166
  127.0 6.1 %fusion.2 = f32[512,576]{0,1:T(8,128)} fusion(bf16[1,3072,576]{1,2,0:T(8,128)(2,1)} %param.27, bf16[512,6144]{1,0:T(8,128)(2,1)} %all-gather.5.cloned.1.call-done), kind=kOutput, calls=%fused_computation.6 | convolution fusion | flops 1811939328 | bytes 7864320 | tf_op jit(solution)/shard_map/dot_general | solution.py:43
  133.1 3.1 fusion.7
  136.2 11.1 %fusion = f32[512,3072]{1,0:T(8,128)} fusion(bf16[1,3072,576]{1,2,0:T(8,128)(2,1)} %param.27, f32[512,576]{0,1:T(8,128)} %fusion.7, bf16[1,3072,576]{1,2,0:T(8,128)(2,1)S(1)} %copy-done, bf16[512,6144]{1,0:T(8,128)(2,1)} %all-gather.5.cloned.1.call-done, f32[512,576]{0,1:T(8,128)} %fusion.2), kind=kOutput, calls=%fused_computation.4 | convolution fusion | flops 3626827776 | bytes 18874368 | tf_op jit(solution)/shard_map/dot_general | solution.py:53
  147.3 6.8 %add_convert_fusion = bf16[512,3072]{1,0:T(8,128)(2,1)} fusion(f32[512,3072]{1,0:T(8,128)} %fusion, bf16[1,3072,576]{1,2,0:T(8,128)(2,1)S(1)} %copy-done, f32[512,576]{0,1:T(8,128)} %fusion.7, f32[512,576]{0,1:T(8,128)} %fusion.2), kind=kOutput, calls=%fused_computation.3 | convolution fusion | flops 1816854528 | bytes 15335424 | tf_op jit(solution)/shard_map/dot_general | solution.py:56
  154.1 7.2 %convert_element_type.79 = bf16[8,32,2,3072]{3,2,1,0:T(2,128)(2,1)} reshape(bf16[512,3072]{1,0:T(8,128)(2,1)} %add_convert_fusion) | data formatting | bytes 6291456 | tf_op jit(solution)/shard_map/convert_element_type | solution.py:170
  161.3 4.4 %copy.34 = bf16[8,32,2,3072]{3,1,2,0:T(8,128)(2,1)} copy(bf16[8,32,2,3072]{3,2,1,0:T(2,128)(2,1)} %convert_element_type.79) | data formatting | bytes 6291456 | tf_op jit(solution)/shard_map/convert_element_type | solution.py:170
  165.7 45.8 %reduce-scatter.2.cloned.1.call-done = bf16[1,32,2,3072]{3,1,2,0:T(8,128)(2,1)} async-done(((bf16[8,32,2,3072]{3,1,2,0:T(8,128)(2,1)}), bf16[1,32,2,3072]{3,1,2,0:T(8,128)(2,1)}) %reduce-scatter.2.cloned.1.call-update) | async-done | bytes 393232 | tf_op jit(solution)/shard_map/reduce_scatter | solution.py:169
  213.7 7.3 %all-to-all-start.1 = ((bf16[32,2,3072]{2,1,0:T(2,128)(2,1)}), bf16[32,2,3072]{2,1,0:T(2,128)(2,1)}, u32[]{:S(2)}, u32[]{:S(2)}) async-start(bf16[32,2,3072]{2,1,0:T(2,128)(2,1)} %copy.35), calls=%async_computation.2 | async-start | bytes 786432 | tf_op jit(solution)/shard_map/all_to_all | solution.py:172
  223.7 6.3 %all-to-all-done.1 = bf16[32,2,3072]{2,1,0:T(2,128)(2,1)} async-done(((bf16[32,2,3072]{2,1,0:T(2,128)(2,1)}), bf16[32,2,3072]{2,1,0:T(2,128)(2,1)}, u32[]{:S(2)}, u32[]{:S(2)}) %all-to-all-start.1) | async-done | bytes 393248 | tf_op jit(solution)/shard_map/all_to_all | solution.py:172
  240.6 16.3 %all-reduce = f32[8]{0:T(128)} all-reduce(f32[8]{0:T(128)S(1)} %dynamic-update-slice), channel_id=1, replica_groups=mesh['ctx'=8,'exp'=32] {'ctx'}, use_global_device_ids=true, to_apply=%add | all-reduce | flops 8 | bytes 64
  259.1 27.3 %all-gather = f32[1024,128]{1,0:T(8,128)} all-gather(f32[128,128]{1,0:T(8,128)S(1)} %fusion.53), channel_id=2, replica_groups=mesh['ctx'=8,'exp'=32] {'ctx'}, dimensions={0}, use_global_device_ids=true | all-gather | bytes 589824 | tf_op jit(solution)/shard_map/all_gather | solution.py:12
  287.0 4.0 %convolution_convert_fusion.1 = bf16[768,128]{1,0:T(8,128)(2,1)S(1)} fusion(bf16[768,3072]{1,0:T(8,128)(2,1)} %all-gather.7.cloned.1.call-done, bf16[128,3072]{1,0:T(8,128)(2,1)} %param.26), kind=kOutput, calls=%fused_computation.42 | convolution fusion | flops 604078080 | bytes 5701632 | tf_op jit(solution)/shard_map/dot_general | solution.py:188
  293.2 3.2 fusion.22
  298.1 49.7 %all-gather.1 = f32[1024,128]{1,0:T(8,128)} all-gather(f32[128,128]{1,0:T(8,128)S(1)} %convolution_multiply_fusion.3), channel_id=3, replica_groups=mesh['ctx'=8,'exp'=32] {'ctx'}, dimensions={0}, use_global_device_ids=true | all-gather | bytes 589824 | tf_op jit(solution)/shard_map/all_gather | solution.py:12
  348.4 23.6 %while.27 = (s32[]{:T(128)}, f32[128,128]{1,0:T(8,128)}, s32[]{:T(128)}, f32[8]{0:T(128)}, f32[8,128,128]{2,1,0:T(8,128)}, /*index=5*/s32[]{:T(128)}, s32[]{:T(128)}, s32[]{:T(128)}, s32[]{:T(128)}) while((s32[]{:T(128)}, f32[128,128]{1,0:T(8,128)}, s32[]{:T(128)}, f32[8]{0:T(128)}, f32[8,128,128]{2,1,0:T(8,128)}, /*index=5*/s32[]{:T(128)}, ...), condition=%wide.region_11.12_spmd, body=%wide.region_10.11_spmd.sunk | while | flops 32774 | bytes 196767 | solution.py:21
  349.6 2.2 bitcast_add_fusion.5
  356.4 2.2 bitcast_add_fusion.5
  375.6 2.5 fusion.41
  (83 shorter events, 60.3 us)
Async XLA Ops:
  7.2 129.1 %copy-start = (bf16[1,3072,576]{1,2,0:T(8,128)(2,1)S(1)}, bf16[1,3072,576]{1,2,0:T(8,128)(2,1)}, u32[]{:S(2)}) copy-start(bf16[1,3072,576]{1,2,0:T(8,128)(2,1)} %param.28) | copy-start | bytes 10616836
  7.2 119.8 %all-gather.5.cloned.1.call-start = ((), (), s32[]{:S(2)}) async-start(), calls=%async_computation.3 | async-start | bytes 7077888 | tf_op jit(solution)/shard_map/all_gather | solution.py:166
  52.2 159.4 %reduce-scatter.2.cloned.1.call-start = ((), (), s32[]{:S(2)}) async-start(), calls=%async_computation.4 | async-start | bytes 3538944 | tf_op jit(solution)/shard_map/reduce_scatter | solution.py:169
  127.0 6.1 %copy-start.8 = (bf16[512,6144]{1,0:T(8,128)(2,1)S(1)}, bf16[512,6144]{1,0:T(8,128)(2,1)}, u32[]{:S(2)}) copy-start(bf16[512,6144]{1,0:T(8,128)(2,1)} %all-gather.5.cloned.1.call-done) | copy-start | bytes 18874372
  127.0 6.1 %copy-start.9 = (bf16[1,576,3072]{2,1,0:T(8,128)(2,1)S(1)}, bf16[1,576,3072]{2,1,0:T(8,128)(2,1)}, u32[]{:S(2)}) copy-start(bf16[1,576,3072]{2,1,0:T(8,128)(2,1)} %param.29) | copy-start | bytes 10616836
  165.7 67.5 %copy-start.7 = (f32[3072]{0:T(1024)S(1)}, f32[3072]{0:T(1024)}, u32[]{:S(2)}) copy-start(f32[3072]{0:T(1024)} %param.22) | copy-start | bytes 36868
  213.7 16.3 %all-to-all-start.1 = ((bf16[32,2,3072]{2,1,0:T(2,128)(2,1)}), bf16[32,2,3072]{2,1,0:T(2,128)(2,1)}, u32[]{:S(2)}, u32[]{:S(2)}) async-start(bf16[32,2,3072]{2,1,0:T(2,128)(2,1)} %copy.35), calls=%async_computation.2 | async-start | bytes 786432 | tf_op jit(solution)/shard_map/all_to_all | solution.py:172
  221.0 66.0 %all-gather.7.cloned.1.call-start = ((), (), s32[]{:S(2)}) async-start(), calls=%async_computation.5 | async-start | bytes 4866048 | tf_op jit(solution)/shard_map/all_gather | solution.py:189
  287.0 4.7 %copy-start.4 = (bf16[768,128]{1,0:T(8,128)(2,1)S(1)}, bf16[768,128]{1,0:T(8,128)(2,1)}, u32[]{:S(2)}) copy-start(bf16[768,128]{1,0:T(8,128)(2,1)} %param.19) | copy-start | bytes 589828
  291.0 0.7 copy-start.5
  372.0 6.0 %copy-start.2 = (f32[128,128]{1,0:T(8,128)S(1)}, f32[128,128]{1,0:T(8,128)}, u32[]{:S(2)}) copy-start(f32[128,128]{1,0:T(8,128)} %get-tuple-element.131) | copy-start | bytes 196612
  372.0 6.0 %copy-start.6 = (bf16[768,128]{1,0:T(8,128)(2,1)S(1)}, bf16[768,128]{1,0:T(8,128)(2,1)}, u32[]{:S(2)}) copy-start(bf16[768,128]{1,0:T(8,128)(2,1)} %copy-done.5) | copy-start | bytes 589828
  372.0 6.4 %copy-start.1 = (bf16[768,768]{1,0:T(8,128)(2,1)S(1)}, bf16[768,768]{1,0:T(8,128)(2,1)}, u32[]{:S(2)}) copy-start(bf16[768,768]{1,0:T(8,128)(2,1)} %multiply_convert_fusion.1) | copy-start | bytes 3538948
  372.0 6.4 %copy-start.3 = (bf16[768,128]{1,0:T(8,128)(2,1)S(1)}, bf16[768,128]{1,0:T(8,128)(2,1)}, u32[]{:S(2)}) copy-start(bf16[768,128]{1,0:T(8,128)(2,1)} %param.18) | copy-start | bytes 589828
Sparse Core Ops, SparseCore 0:
  52.3 74.6 all-gather.4
  165.9 45.6 reduce-scatter.1
  236.2 48.4 all-gather.6
where the time goes:
time: 388 us; the launch traced here: 386 us
  waiting for transfers between devices  127 us (33%)
  blocking collectives  114 us (29%)
  matrix products  50 us (13%)
  local copies, waits for them, and re-layouts  45.2 us (12%)
  other arithmetic  27.8 us (7%)
  between operations  14.5 us (4%)
  starting transfers between devices  7.6 us (2%)
    all_gather x2, blocking collectives, prefix(): gathered = jax.tree.map(lambda a: lax.all_gather(a, axis), part)  77 us
    all_gather x1, waiting for transfers between devices, body(): lax.all_gather(arrived, 'ctx', axis=0, tiled=True)  74.6 us
    reduce_scatter x1, waiting for transfers between devices, body(): lax.psum_scatter(partials.astype(jnp.bfloat16), 'ctx', scatter_dimension=...  45.8 us
    all_to_all x1, blocking collectives, body(): lax.all_to_all(outgoing, 'exp', split_axis=0, concat_axis=0, tiled=True)  20.9 us
    unnamed x1, blocking collectives  16.3 us
    add x7, other arithmetic, chain_link(): return (earlier[0] * following[0], following[0] * earlier[1] + following[1])  15.1 us
    convert_element_type x2, local copies, waits for them, and re-layouts, body(): partials.astype(jnp.bfloat16)  11.6 us
    dot_general x1, matrix products, expert_rows(): lax.dot_general(gate_grad, gate_mat, (((1,), (1,)), ((), ())), preferred_...  11.1 us
  transfers between devices with their start and end apart: 4, of which 3 were waited for; matrix products, arithmetic and copies ran while one was open for 2% of the time, Pallas kernels for 0%

commit v1 on v0

--- a/solution.py
+++ b/solution.py
@@ -163,7 +163,18 @@
         exp_count * capacity, 2 * features
     )
     partials = expert_rows(
-        lax.all_gather(arrived, "ctx", axis=0, tiled=True), gate_mat, up_mat, down_mat
+        jnp.concatenate(
+            jax.lax.all_to_all(
+                jnp.stack([arrived for _ in range(jax.lax.axis_size("ctx"))], 0),
+                axis_name="ctx",
+                split_axis=0,
+                concat_axis=0,
+            ),
+            0,
+        ),
+        gate_mat,
+        up_mat,
+        down_mat,
     )
     partials = partials.reshape(ctx_count, exp_count, capacity, features)
     summed = lax.psum_scatter(

time: 388 us -> 459 us (1.18)
  blocking collectives: 114 us -> 264 us
  waiting for transfers between devices: 127 us -> 47.2 us
    all_to_all x0 -> x1, blocking collectives: none -> 150 us  [body(): jax.lax.all_to_all(jnp.stack([arrived for _ in range(jax.lax.axis_size('c...]
    all_gather x1 -> x0, waiting for transfers between devices: 74.6 us -> none  [body(): lax.all_gather(arrived, 'ctx', axis=0, tiled=True)]
    reduce_scatter x1, waiting for transfers between devices: 45.8 us -> 40.9 us  [body(): lax.psum_scatter(partials.astype(jnp.bfloat16), 'ctx', scatter_dimension=...]
    another operation x1 -> x3, local copies, waits for them, and re-layouts: 0.12 us -> 4.97 us  [the longest x2 4.85 us: body(): jnp.stack([arrived for _ in range(jax.lax.axis_size('ctx'))], 0)]
  transfers between devices with their start and end apart: 4 -> 3, of which waited for: 3 -> 2; matrix products, arithmetic and copies ran while one was open for 2% -> 2% of each run, Pallas kernels for 0% -> 0%
where the time goes in v1:
time: 459 us; the launch traced here: 457 us
  blocking collectives  264 us (58%)
  local copies, waits for them, and re-layouts  48.7 us (11%)
  waiting for transfers between devices  47.2 us (10%)
  matrix products  47 us (10%)
  other arithmetic  27.7 us (6%)
  between operations  14.8 us (3%)
  starting transfers between devices  7.51 us (2%)
    all_to_all x1, blocking collectives, body(): jax.lax.all_to_all(jnp.stack([arrived for _ in range(jax.lax.axis_size('c...  150 us
    all_gather x2, blocking collectives, prefix(): gathered = jax.tree.map(lambda a: lax.all_gather(a, axis), part)  77.1 us
    reduce_scatter x1, waiting for transfers between devices, body(): lax.psum_scatter(partials.astype(jnp.bfloat16), 'ctx', scatter_dimension=...  40.9 us
    all_to_all x1, blocking collectives, body(): lax.all_to_all(outgoing, 'exp', split_axis=0, concat_axis=0, tiled=True)  20.9 us
    unnamed x1, blocking collectives  16.1 us
    add x7, other arithmetic, chain_link(): return (earlier[0] * following[0], following[0] * earlier[1] + following[1])  15.1 us
    convert_element_type x2, local copies, waits for them, and re-layouts, body(): partials.astype(jnp.bfloat16)  11.7 us
    dot_general x1, matrix products, expert_rows(): lax.dot_general(gate_grad, gate_mat, (((1,), (1,)), ((), ())), preferred_...  11.1 us
  transfers between devices with their start and end apart: 3, of which 2 were waited for; matrix products, arithmetic and copies ran while one was open for 2% of the time, Pallas kernels for 0%

profile of v1, /device:TPU:2, one launch (start us, length us, event | category | flops | bytes accessed | tf_op | source)
XLA Modules:
  0.0 457.3 jit_solution(12713695408041742184)
XLA Ops:
  18.4 2.3 mul.203
  23.2 2.2 convolution_convert_fusion
  25.4 2.9 reshape.143
  28.3 20.9 %all_to_all.15 = bf16[32,2,6144]{2,1,0:T(2,128)(2,1)} all-to-all(bf16[32,2,6144]{2,1,0:T(2,128)(2,1)} %reshape.143), channel_id=1, replica_groups=mesh['ctx'=8,'exp'=32] {'exp'}, dimensions={0} | all-to-all | bytes 1572864 | tf_op jit(solution)/shard_map/all_to_all | solution.py:162
  49.2 3.0 stack_reshape.2
  54.0 150.1 %all_to_all.16 = bf16[8,64,6144]{2,1,0:T(8,128)(2,1)S(1)} all-to-all(bf16[8,64,6144]{2,1,0:T(8,128)(2,1)S(1)} %stack.3), channel_id=1, replica_groups=mesh['ctx'=8,'exp'=32] {'ctx'}, dimensions={0} | all-to-all | bytes 12582912 | tf_op jit(solution)/shard_map/all_to_all | solution.py:167
  204.2 3.0 fusion.2
  208.8 3.1 fusion.7
  211.9 11.1 %fusion = f32[512,3072]{1,0:T(8,128)} fusion(bf16[1,3072,576]{1,2,0:T(8,128)(2,1)} %param.27, f32[512,576]{0,1:T(8,128)} %fusion.7, bf16[1,3072,576]{1,2,0:T(8,128)(2,1)S(1)} %copy-done, bf16[512,6144]{1,0:T(8,128)(2,1)} %bitcast.78, f32[512,576]{0,1:T(8,128)} %fusion.2), kind=kOutput, calls=%fused_computation.4 | convolution fusion | flops 3626827776 | bytes 18874368 | tf_op jit(solution)/shard_map/dot_general | solution.py:53
  223.0 6.9 %add_convert_fusion = bf16[512,3072]{1,0:T(8,128)(2,1)} fusion(f32[512,3072]{1,0:T(8,128)} %fusion, bf16[1,3072,576]{1,2,0:T(8,128)(2,1)S(1)} %copy-done, f32[512,576]{0,1:T(8,128)} %fusion.7, f32[512,576]{0,1:T(8,128)} %fusion.2), kind=kOutput, calls=%fused_computation.3 | convolution fusion | flops 1816854528 | bytes 15335424 | tf_op jit(solution)/shard_map/dot_general | solution.py:56
  229.8 7.2 %convert_element_type.79 = bf16[8,32,2,3072]{3,2,1,0:T(2,128)(2,1)} reshape(bf16[512,3072]{1,0:T(8,128)(2,1)} %add_convert_fusion) | data formatting | bytes 6291456 | tf_op jit(solution)/shard_map/convert_element_type | solution.py:181
  237.1 4.4 copy.34
  241.5 40.9 %reduce-scatter.2.cloned.1.call-done = bf16[1,32,2,3072]{3,1,2,0:T(8,128)(2,1)} async-done(((bf16[8,32,2,3072]{3,1,2,0:T(8,128)(2,1)}), bf16[1,32,2,3072]{3,1,2,0:T(8,128)(2,1)}) %reduce-scatter.2.cloned.1.call-update) | async-done | bytes 393232 | tf_op jit(solution)/shard_map/reduce_scatter | solution.py:180
  284.5 7.4 %all-to-all-start.2 = ((bf16[32,2,3072]{2,1,0:T(2,128)(2,1)}), bf16[32,2,3072]{2,1,0:T(2,128)(2,1)}, u32[]{:S(2)}, u32[]{:S(2)}) async-start(bf16[32,2,3072]{2,1,0:T(2,128)(2,1)} %copy.35), calls=%async_computation.3 | async-start | bytes 786432 | tf_op jit(solution)/shard_map/all_to_all | solution.py:183
  294.6 6.3 %all-to-all-done.2 = bf16[32,2,3072]{2,1,0:T(2,128)(2,1)} async-done(((bf16[32,2,3072]{2,1,0:T(2,128)(2,1)}), bf16[32,2,3072]{2,1,0:T(2,128)(2,1)}, u32[]{:S(2)}, u32[]{:S(2)}) %all-to-all-start.2) | async-done | bytes 393248 | tf_op jit(solution)/shard_map/all_to_all | solution.py:183
  311.6 16.1 %all-reduce = f32[8]{0:T(128)} all-reduce(f32[8]{0:T(128)S(1)} %dynamic-update-slice), channel_id=1, replica_groups=mesh['ctx'=8,'exp'=32] {'ctx'}, use_global_device_ids=true, to_apply=%add | all-reduce | flops 8 | bytes 64
  329.9 27.3 %all-gather = f32[1024,128]{1,0:T(8,128)} all-gather(f32[128,128]{1,0:T(8,128)S(1)} %fusion.53), channel_id=2, replica_groups=mesh['ctx'=8,'exp'=32] {'ctx'}, dimensions={0}, use_global_device_ids=true | all-gather | bytes 589824 | tf_op jit(solution)/shard_map/all_gather | solution.py:12
  357.8 4.0 convolution_convert_fusion.1
  364.0 3.2 fusion.22
  368.9 49.8 %all-gather.1 = f32[1024,128]{1,0:T(8,128)} all-gather(f32[128,128]{1,0:T(8,128)S(1)} %convolution_multiply_fusion.3), channel_id=3, replica_groups=mesh['ctx'=8,'exp'=32] {'ctx'}, dimensions={0}, use_global_device_ids=true | all-gather | bytes 589824 | tf_op jit(solution)/shard_map/all_gather | solution.py:12
  419.3 23.6 %while.27 = (s32[]{:T(128)}, f32[128,128]{1,0:T(8,128)}, s32[]{:T(128)}, f32[8]{0:T(128)}, f32[8,128,128]{2,1,0:T(8,128)}, /*index=5*/s32[]{:T(128)}, s32[]{:T(128)}, s32[]{:T(128)}, s32[]{:T(128)}) while((s32[]{:T(128)}, f32[128,128]{1,0:T(8,128)}, s32[]{:T(128)}, f32[8]{0:T(128)}, f32[8,128,128]{2,1,0:T(8,128)}, /*index=5*/s32[]{:T(128)}, ...), condition=%wide.region_11.12_spmd, body=%wide.region_10.11_spmd.sunk | while | flops 32774 | bytes 196767 | solution.py:21
  420.5 2.2 bitcast_add_fusion.5
  423.9 2.2 bitcast_add_fusion.5
  446.4 2.5 fusion.41
  (84 shorter events, 63.6 us)
Async XLA Ops:
  7.2 204.7 %copy-start = (bf16[1,3072,576]{1,2,0:T(8,128)(2,1)S(1)}, bf16[1,3072,576]{1,2,0:T(8,128)(2,1)}, u32[]{:S(2)}) copy-start(bf16[1,3072,576]{1,2,0:T(8,128)(2,1)} %param.28) | copy-start | bytes 10616836
  7.2 275.2 %reduce-scatter.2.cloned.1.call-start = ((), (), s32[]{:S(2)}) async-start(), calls=%async_computation.4 | async-start | bytes 3538944 | tf_op jit(solution)/shard_map/reduce_scatter | solution.py:180
  54.0 150.2 %copy-start.10 = (bf16[1,3072,576]{1,2,0:T(8,128)(2,1)S(1)}, bf16[1,3072,576]{1,2,0:T(8,128)(2,1)}, u32[]{:S(2)}) copy-start(bf16[1,3072,576]{1,2,0:T(8,128)(2,1)} %param.27) | copy-start | bytes 10616836
  204.2 3.7 copy-start.1
  204.2 4.6 %copy-start.9 = (bf16[1,576,3072]{2,1,0:T(8,128)(2,1)S(1)}, bf16[1,576,3072]{2,1,0:T(8,128)(2,1)}, u32[]{:S(2)}) copy-start(bf16[1,576,3072]{2,1,0:T(8,128)(2,1)} %param.29) | copy-start | bytes 10616836
  241.5 62.7 %copy-start.8 = (f32[3072]{0:T(1024)S(1)}, f32[3072]{0:T(1024)}, u32[]{:S(2)}) copy-start(f32[3072]{0:T(1024)} %param.22) | copy-start | bytes 36868
  284.5 16.5 %all-to-all-start.2 = ((bf16[32,2,3072]{2,1,0:T(2,128)(2,1)}), bf16[32,2,3072]{2,1,0:T(2,128)(2,1)}, u32[]{:S(2)}, u32[]{:S(2)}) async-start(bf16[32,2,3072]{2,1,0:T(2,128)(2,1)} %copy.35), calls=%async_computation.3 | async-start | bytes 786432 | tf_op jit(solution)/shard_map/all_to_all | solution.py:183
  292.0 65.9 %all-gather.4.cloned.1.call-start = ((), (), s32[]{:S(2)}) async-start(), calls=%async_computation.5 | async-start | bytes 4866048 | tf_op jit(solution)/shard_map/all_gather | solution.py:200
  357.8 4.7 %copy-start.5 = (bf16[768,128]{1,0:T(8,128)(2,1)S(1)}, bf16[768,128]{1,0:T(8,128)(2,1)}, u32[]{:S(2)}) copy-start(bf16[768,128]{1,0:T(8,128)(2,1)} %param.19) | copy-start | bytes 589828
  361.8 0.7 copy-start.6
  442.9 6.0 %copy-start.3 = (f32[128,128]{1,0:T(8,128)S(1)}, f32[128,128]{1,0:T(8,128)}, u32[]{:S(2)}) copy-start(f32[128,128]{1,0:T(8,128)} %get-tuple-element.131) | copy-start | bytes 196612
  442.9 6.0 %copy-start.7 = (bf16[768,128]{1,0:T(8,128)(2,1)S(1)}, bf16[768,128]{1,0:T(8,128)(2,1)}, u32[]{:S(2)}) copy-start(bf16[768,128]{1,0:T(8,128)(2,1)} %copy-done.6) | copy-start | bytes 589828
  442.9 6.4 %copy-start.2 = (bf16[768,768]{1,0:T(8,128)(2,1)S(1)}, bf16[768,768]{1,0:T(8,128)(2,1)}, u32[]{:S(2)}) copy-start(bf16[768,768]{1,0:T(8,128)(2,1)} %multiply_convert_fusion.1) | copy-start | bytes 3538948
  442.9 6.4 %copy-start.4 = (bf16[768,128]{1,0:T(8,128)(2,1)S(1)}, bf16[768,128]{1,0:T(8,128)(2,1)}, u32[]{:S(2)}) copy-start(bf16[768,128]{1,0:T(8,128)(2,1)} %param.18) | copy-start | bytes 589828
Sparse Core Ops, SparseCore 0:
  241.6 40.6 reduce-scatter.1
  307.2 48.2 all-gather.3
